TPU v7x, 256 devices: a whole 4x4x8 slice. The times are simulated.
256 devices in a mesh: samp: 8 (over z), snp: 32 (over x, y, core).
Axes of the slice: x: 4, y: 4, z: 8, core: 2. Of those that a mesh axis runs over, the one named last changes fastest.
Arguments:
- genotypes: bfloat16 [16384, 65536], P('samp', 'snp'), may hold values from 0 to 3, as said below
- frequency: float32 [65536], P('snp'), may hold values from 0.03 to 0.97
- seed_matrix: float32 [32, 65536], P(None, 'snp'), may hold values from -6 to 6
Outputs:
- sample_basis: bfloat16 [32, 16384], P(None, 'samp')
- snp_basis: bfloat16 [32, 65536], P(None, 'snp')
Inputs may be any that keep to these rules, and one draw needn't show every extreme that they name: `genotypes`: dosages 0, 1, 2; the value 3 marks a missing call.
All inputs are finite; a program needn't handle non-finite values.
Results may differ from a plain program's by a relative error of at most 0.025.
Values may be sent and summed in bfloat16 or wider, within the bound.
A program may use at most 64 MiB of HBM per device.

v0:
```python
import jax
import jax.numpy as jnp
from jax import lax
from jax.sharding import PartitionSpec as P

ITERS = 6


def padded_to(lines, length):
    spare = -len(lines) % length
    return jnp.pad(lines, [(0, spare)] + [(0, 0)] * (lines.ndim - 1))


def joined_along(pieces, dim):
    pieces = jnp.moveaxis(pieces, 0, dim)
    lengths = pieces.shape
    return pieces.reshape(*lengths[:dim], lengths[dim] * lengths[dim + 1], *lengths[dim + 2 :])


def from_everyone(value, axis):
    copies = jnp.broadcast_to(value, (lax.axis_size(axis), *value.shape))
    return lax.all_to_all(copies, axis, split_axis=0, concat_axis=0, tiled=True)


def gather_directly(value, axis, dim):
    return joined_along(from_everyone(value, axis), dim)


def split_up(value, dim, length):
    lengths = value.shape
    pieces = value.reshape(*lengths[:dim], length, lengths[dim] // length, *lengths[dim + 1 :])
    return jnp.moveaxis(pieces, dim, 0)


def sum_at_owner(value, axis, dim):
    length = lax.axis_size(axis)
    pieces = lax.all_to_all(split_up(value, dim, length), axis, 0, 0, tiled=True)
    return jnp.sum(pieces.astype(jnp.float32), axis=0)


def total_of(value, axes):
    lines = value.reshape(-1, value.shape[-1])
    padded = padded_to(lines, lax.axis_size(axes))
    whole = gather_directly(sum_at_owner(padded, axes, 0).astype(jnp.bfloat16), axes, 0)
    return lax.slice_in_dim(whole, 0, len(lines)).reshape(value.shape).astype(jnp.float32)


def taken_together(value, axis):
    everything = from_everyone(value, axis)
    return jnp.sum(everything, axis=0)


def over_copies(value, axis):
    everything = from_everyone(value, axis)
    return jnp.sum(everything.astype(jnp.float32), axis=0)


def standardize(block, freq):
    values = block.astype(jnp.float32)
    scale = lax.rsqrt(2.0 * freq * (1.0 - freq))
    return jnp.where(block < 3, (values - 2.0 * freq) * scale, jnp.float32(0.0)).astype(
        jnp.bfloat16
    )


def gram_of(rows):
    return jnp.dot(rows, rows.T, precision=lax.Precision.HIGHEST)


def apply_factor(rows, gram_total, count):
    lower = jnp.linalg.cholesky(gram_total / count)
    return jax.scipy.linalg.solve_triangular(lower, rows, lower=True)


def sample_side(left, xmat, count):
    partial_rows = lax.dot_general(
        left.astype(jnp.bfloat16),
        xmat,
        (((1,), (1,)), ((), ())),
        preferred_element_type=jnp.float32,
    )
    summed = total_of(partial_rows.astype(jnp.bfloat16), "snp")
    gram_total = taken_together(gram_of(summed), "samp")
    return apply_factor(summed, gram_total, count).astype(jnp.bfloat16)


def snp_side(qmat, xmat, count):
    partial_rows = jnp.dot(qmat, xmat, preferred_element_type=jnp.float32)
    summed = over_copies(partial_rows.astype(jnp.bfloat16), "samp").astype(jnp.float32)
    gram_total = taken_together(gram_of(summed), "snp")
    return apply_factor(summed, gram_total, count).astype(jnp.bfloat16)


def per_device(genotypes, frequency, seed_matrix):
    xmat = standardize(genotypes, frequency)
    sample_count = jnp.float32(genotypes.shape[0] * lax.axis_size("samp"))
    snp_count = jnp.float32(genotypes.shape[1] * lax.axis_size("snp"))
    qmat = sample_side(seed_matrix, xmat, sample_count)
    pmat = seed_matrix.astype(jnp.bfloat16)
    for step_index in range(ITERS):
        pmat = snp_side(qmat, xmat, snp_count)
        qmat = sample_side(pmat, xmat, sample_count)
    return (qmat, pmat)


def solution(mesh):
    placed = (P("samp", "snp"), P("snp"), P(None, "snp"))
    return jax.shard_map(
        per_device,
        mesh=mesh,
        in_specs=placed,
        out_specs=(P(None, "samp"), P(None, "snp")),
        check_vma=False,
    )
```

profile of v0, /device:TPU:1, one launch (start us, length us, event | category | flops | bytes accessed | tf_op | source)
XLA Modules:
  0.0 741.6 jit_solution(11161115690895846857)
XLA Ops:
  1.3 9.2 %fusion = bf16[32,1,2048]{2,0,1:T(8,128)(2,1)S(1)} fusion(f32[32,2048]{1,0:T(8,128)} %param.8, bf16[2048,2048]{1,0:T(8,128)(2,1)} %param.6, f32[2048]{0:T(1024)S(1)} %get-tuple-element.5, f32[2048]{0:T(1024)S(1)} %get-tuple-element.4), kind=kOutput, calls=%fused_computation.27 | convolution fusion | flops 293732352 | bytes 8798208 | tf_op jit(solution)/shard_map/dot_general | solution.py:76
  11.8 16.1 %all_to_all.165 = bf16[32,2,1024]{2,1,0:T(2,128)(2,1)S(1)} all-to-all(bf16[32,2,1024]{2,1,0:T(2,128)(2,1)S(1)} %reshape.91), channel_id=1, replica_groups=mesh['samp'=8,'snp'=32] {'snp'}, dimensions={0} | all-to-all | bytes 262144 | tf_op jit(solution)/shard_map/all_to_all | solution.py:37
  29.8 11.2 %all_to_all.166 = bf16[32,2,1024]{2,1,0:T(2,128)(2,1)S(1)} all-to-all(bf16[32,2,1024]{2,1,0:T(2,128)(2,1)S(1)} %reshape.93), channel_id=1, replica_groups=mesh['samp'=8,'snp'=32] {'snp'}, dimensions={0} | all-to-all | bytes 262144 | tf_op jit(solution)/shard_map/all_to_all | solution.py:22
  41.5 15.0 %all_to_all.167 = f32[8,1,1024]{2,1,0:T(1,128)S(1)} all-to-all(f32[8,1,1024]{2,1,0:T(1,128)S(1)} %reshape.95), channel_id=1, replica_groups=mesh['samp'=8,'snp'=32] {'samp'}, dimensions={0} | all-to-all | bytes 65536 | tf_op jit(solution)/shard_map/all_to_all | solution.py:22
  65.2 9.2 %convolution_convert_fusion.24 = bf16[32,2048]{1,0:T(8,128)(2,1)S(1)} fusion(bf16[32,2048]{1,0:T(8,128)(2,1)S(1)} %convolution_convert_fusion.12, bf16[2048,2048]{1,0:T(8,128)(2,1)} %param.6, f32[2048]{0:T(1024)S(1)} %get-tuple-element.5, f32[2048]{0:T(1024)S(1)} %get-tuple-element.4), kind=kOutput, calls=%fused_computation.25 | convolution fusion | flops 293666816 | bytes 8667136 | tf_op jit(solution)/shard_map/dot_general | solution.py:88
  74.6 28.8 %all_to_all.168 = bf16[8,32,2048]{2,1,0:T(8,128)(2,1)S(1)} all-to-all(bf16[8,32,2048]{2,1,0:T(8,128)(2,1)S(1)} %broadcast_in_dim.88), channel_id=1, replica_groups=mesh['samp'=8,'snp'=32] {'samp'}, dimensions={0} | all-to-all | bytes 2097152 | tf_op jit(solution)/shard_map/all_to_all | solution.py:22
  104.2 14.5 %all_to_all.169 = f32[32,1,1024]{2,1,0:T(1,128)S(1)} all-to-all(f32[32,1,1024]{2,1,0:T(1,128)S(1)} %reshape.97), channel_id=1, replica_groups=mesh['samp'=8,'snp'=32] {'snp'}, dimensions={0} | all-to-all | bytes 262144 | tf_op jit(solution)/shard_map/all_to_all | solution.py:22
  120.1 2.9 cholesky.220
  127.2 7.7 %fusion.1 = bf16[32,1,2048]{2,0,1:T(8,128)(2,1)S(1)} fusion(bf16[32,2048]{1,0:T(8,128)(2,1)S(1)} %convolution_convert_fusion.11, bf16[2048,2048]{1,0:T(8,128)(2,1)} %param.6, f32[2048]{0:T(1024)S(1)} %get-tuple-element.5, f32[2048]{0:T(1024)S(1)} %get-tuple-element.4), kind=kOutput, calls=%fused_computation.28 | convolution fusion | flops 293666816 | bytes 8667136 | tf_op jit(solution)/shard_map/dot_general | solution.py:76
  135.6 11.3 %all_to_all.170 = bf16[32,2,1024]{2,1,0:T(2,128)(2,1)S(1)} all-to-all(bf16[32,2,1024]{2,1,0:T(2,128)(2,1)S(1)} %reshape.99), channel_id=1, replica_groups=mesh['samp'=8,'snp'=32] {'snp'}, dimensions={0} | all-to-all | bytes 262144 | tf_op jit(solution)/shard_map/all_to_all | solution.py:37
  148.8 11.2 %all_to_all.171 = bf16[32,2,1024]{2,1,0:T(2,128)(2,1)S(1)} all-to-all(bf16[32,2,1024]{2,1,0:T(2,128)(2,1)S(1)} %reshape.101), channel_id=1, replica_groups=mesh['samp'=8,'snp'=32] {'snp'}, dimensions={0} | all-to-all | bytes 262144 | tf_op jit(solution)/shard_map/all_to_all | solution.py:22
  160.6 9.2 %all_to_all.172 = f32[8,1,1024]{2,1,0:T(1,128)S(1)} all-to-all(f32[8,1,1024]{2,1,0:T(1,128)S(1)} %reshape.103), channel_id=1, replica_groups=mesh['samp'=8,'snp'=32] {'samp'}, dimensions={0} | all-to-all | bytes 65536 | tf_op jit(solution)/shard_map/all_to_all | solution.py:22
  178.0 9.2 %convolution_convert_fusion.22 = bf16[32,2048]{1,0:T(8,128)(2,1)S(1)} fusion(bf16[32,2048]{1,0:T(8,128)(2,1)S(1)} %convolution_convert_fusion.10, bf16[2048,2048]{1,0:T(8,128)(2,1)} %param.6, f32[2048]{0:T(1024)S(1)} %get-tuple-element.5, f32[2048]{0:T(1024)S(1)} %get-tuple-element.4), kind=kOutput, calls=%fused_computation.23 | convolution fusion | flops 293666816 | bytes 8667136 | tf_op jit(solution)/shard_map/dot_general | solution.py:88
  187.3 29.0 %all_to_all.173 = bf16[8,32,2048]{2,1,0:T(8,128)(2,1)S(1)} all-to-all(bf16[8,32,2048]{2,1,0:T(8,128)(2,1)S(1)} %broadcast_in_dim.92), channel_id=1, replica_groups=mesh['samp'=8,'snp'=32] {'samp'}, dimensions={0} | all-to-all | bytes 2097152 | tf_op jit(solution)/shard_map/all_to_all | solution.py:22
  217.2 14.0 %all_to_all.174 = f32[32,1,1024]{2,1,0:T(1,128)S(1)} all-to-all(f32[32,1,1024]{2,1,0:T(1,128)S(1)} %reshape.105), channel_id=1, replica_groups=mesh['samp'=8,'snp'=32] {'snp'}, dimensions={0} | all-to-all | bytes 262144 | tf_op jit(solution)/shard_map/all_to_all | solution.py:22
  232.5 2.9 cholesky.242
  239.7 7.7 %fusion.2 = bf16[32,1,2048]{2,0,1:T(8,128)(2,1)S(1)} fusion(bf16[32,2048]{1,0:T(8,128)(2,1)S(1)} %convolution_convert_fusion.9, bf16[2048,2048]{1,0:T(8,128)(2,1)} %param.6, f32[2048]{0:T(1024)S(1)} %get-tuple-element.5, f32[2048]{0:T(1024)S(1)} %get-tuple-element.4), kind=kOutput, calls=%fused_computation.29 | convolution fusion | flops 293666816 | bytes 8667136 | tf_op jit(solution)/shard_map/dot_general | solution.py:76
  248.1 11.3 %all_to_all.175 = bf16[32,2,1024]{2,1,0:T(2,128)(2,1)S(1)} all-to-all(bf16[32,2,1024]{2,1,0:T(2,128)(2,1)S(1)} %reshape.107), channel_id=1, replica_groups=mesh['samp'=8,'snp'=32] {'snp'}, dimensions={0} | all-to-all | bytes 262144 | tf_op jit(solution)/shard_map/all_to_all | solution.py:37
  261.3 11.2 %all_to_all.176 = bf16[32,2,1024]{2,1,0:T(2,128)(2,1)S(1)} all-to-all(bf16[32,2,1024]{2,1,0:T(2,128)(2,1)S(1)} %reshape.109), channel_id=1, replica_groups=mesh['samp'=8,'snp'=32] {'snp'}, dimensions={0} | all-to-all | bytes 262144 | tf_op jit(solution)/shard_map/all_to_all | solution.py:22
  273.0 9.2 %all_to_all.177 = f32[8,1,1024]{2,1,0:T(1,128)S(1)} all-to-all(f32[8,1,1024]{2,1,0:T(1,128)S(1)} %reshape.111), channel_id=1, replica_groups=mesh['samp'=8,'snp'=32] {'samp'}, dimensions={0} | all-to-all | bytes 65536 | tf_op jit(solution)/shard_map/all_to_all | solution.py:22
  290.5 9.2 %convolution_convert_fusion.20 = bf16[32,2048]{1,0:T(8,128)(2,1)S(1)} fusion(bf16[32,2048]{1,0:T(8,128)(2,1)S(1)} %convolution_convert_fusion.8, bf16[2048,2048]{1,0:T(8,128)(2,1)} %param.6, f32[2048]{0:T(1024)S(1)} %get-tuple-element.5, f32[2048]{0:T(1024)S(1)} %get-tuple-element.4), kind=kOutput, calls=%fused_computation.21 | convolution fusion | flops 293666816 | bytes 8667136 | tf_op jit(solution)/shard_map/dot_general | solution.py:88
  299.8 29.0 %all_to_all.178 = bf16[8,32,2048]{2,1,0:T(8,128)(2,1)S(1)} all-to-all(bf16[8,32,2048]{2,1,0:T(8,128)(2,1)S(1)} %broadcast_in_dim.96), channel_id=1, replica_groups=mesh['samp'=8,'snp'=32] {'samp'}, dimensions={0} | all-to-all | bytes 2097152 | tf_op jit(solution)/shard_map/all_to_all | solution.py:22
  329.6 14.0 %all_to_all.179 = f32[32,1,1024]{2,1,0:T(1,128)S(1)} all-to-all(f32[32,1,1024]{2,1,0:T(1,128)S(1)} %reshape.113), channel_id=1, replica_groups=mesh['samp'=8,'snp'=32] {'snp'}, dimensions={0} | all-to-all | bytes 262144 | tf_op jit(solution)/shard_map/all_to_all | solution.py:22
  352.2 7.7 %fusion.3 = bf16[32,1,2048]{2,0,1:T(8,128)(2,1)S(1)} fusion(bf16[32,2048]{1,0:T(8,128)(2,1)S(1)} %convolution_convert_fusion.7, bf16[2048,2048]{1,0:T(8,128)(2,1)} %param.6, f32[2048]{0:T(1024)S(1)} %get-tuple-element.5, f32[2048]{0:T(1024)S(1)} %get-tuple-element.4), kind=kOutput, calls=%fused_computation.30 | convolution fusion | flops 293666816 | bytes 8667136 | tf_op jit(solution)/shard_map/dot_general | solution.py:76
  360.6 11.3 %all_to_all.180 = bf16[32,2,1024]{2,1,0:T(2,128)(2,1)S(1)} all-to-all(bf16[32,2,1024]{2,1,0:T(2,128)(2,1)S(1)} %reshape.115), channel_id=1, replica_groups=mesh['samp'=8,'snp'=32] {'snp'}, dimensions={0} | all-to-all | bytes 262144 | tf_op jit(solution)/shard_map/all_to_all | solution.py:37
  373.8 11.2 %all_to_all.181 = bf16[32,2,1024]{2,1,0:T(2,128)(2,1)S(1)} all-to-all(bf16[32,2,1024]{2,1,0:T(2,128)(2,1)S(1)} %reshape.117), channel_id=1, replica_groups=mesh['samp'=8,'snp'=32] {'snp'}, dimensions={0} | all-to-all | bytes 262144 | tf_op jit(solution)/shard_map/all_to_all | solution.py:22
  385.5 9.2 %all_to_all.182 = f32[8,1,1024]{2,1,0:T(1,128)S(1)} all-to-all(f32[8,1,1024]{2,1,0:T(1,128)S(1)} %reshape.119), channel_id=1, replica_groups=mesh['samp'=8,'snp'=32] {'samp'}, dimensions={0} | all-to-all | bytes 65536 | tf_op jit(solution)/shard_map/all_to_all | solution.py:22
  403.0 9.2 %convolution_convert_fusion.18 = bf16[32,2048]{1,0:T(8,128)(2,1)S(1)} fusion(bf16[32,2048]{1,0:T(8,128)(2,1)S(1)} %convolution_convert_fusion.6, bf16[2048,2048]{1,0:T(8,128)(2,1)} %param.6, f32[2048]{0:T(1024)S(1)} %get-tuple-element.5, f32[2048]{0:T(1024)S(1)} %get-tuple-element.4), kind=kOutput, calls=%fused_computation.19 | convolution fusion | flops 293666816 | bytes 8667136 | tf_op jit(solution)/shard_map/dot_general | solution.py:88
  412.3 29.0 %all_to_all.183 = bf16[8,32,2048]{2,1,0:T(8,128)(2,1)S(1)} all-to-all(bf16[8,32,2048]{2,1,0:T(8,128)(2,1)S(1)} %broadcast_in_dim.100), channel_id=1, replica_groups=mesh['samp'=8,'snp'=32] {'samp'}, dimensions={0} | all-to-all | bytes 2097152 | tf_op jit(solution)/shard_map/all_to_all | solution.py:22
  442.2 14.2 %all_to_all.184 = f32[32,1,1024]{2,1,0:T(1,128)S(1)} all-to-all(f32[32,1,1024]{2,1,0:T(1,128)S(1)} %reshape.121), channel_id=1, replica_groups=mesh['samp'=8,'snp'=32] {'snp'}, dimensions={0} | all-to-all | bytes 262144 | tf_op jit(solution)/shard_map/all_to_all | solution.py:22
  464.9 7.7 %fusion.4 = bf16[32,1,2048]{2,0,1:T(8,128)(2,1)S(1)} fusion(bf16[32,2048]{1,0:T(8,128)(2,1)S(1)} %convolution_convert_fusion.5, bf16[2048,2048]{1,0:T(8,128)(2,1)} %param.6, f32[2048]{0:T(1024)S(1)} %get-tuple-element.5, f32[2048]{0:T(1024)S(1)} %get-tuple-element.4), kind=kOutput, calls=%fused_computation.31 | convolution fusion | flops 293666816 | bytes 8667136 | tf_op jit(solution)/shard_map/dot_general | solution.py:76
  473.3 11.3 %all_to_all.185 = bf16[32,2,1024]{2,1,0:T(2,128)(2,1)S(1)} all-to-all(bf16[32,2,1024]{2,1,0:T(2,128)(2,1)S(1)} %reshape.123), channel_id=1, replica_groups=mesh['samp'=8,'snp'=32] {'snp'}, dimensions={0} | all-to-all | bytes 262144 | tf_op jit(solution)/shard_map/all_to_all | solution.py:37
  486.5 11.2 %all_to_all.186 = bf16[32,2,1024]{2,1,0:T(2,128)(2,1)S(1)} all-to-all(bf16[32,2,1024]{2,1,0:T(2,128)(2,1)S(1)} %reshape.125), channel_id=1, replica_groups=mesh['samp'=8,'snp'=32] {'snp'}, dimensions={0} | all-to-all | bytes 262144 | tf_op jit(solution)/shard_map/all_to_all | solution.py:22
  498.2 9.2 %all_to_all.187 = f32[8,1,1024]{2,1,0:T(1,128)S(1)} all-to-all(f32[8,1,1024]{2,1,0:T(1,128)S(1)} %reshape.127), channel_id=1, replica_groups=mesh['samp'=8,'snp'=32] {'samp'}, dimensions={0} | all-to-all | bytes 65536 | tf_op jit(solution)/shard_map/all_to_all | solution.py:22
  515.7 9.2 %convolution_convert_fusion.16 = bf16[32,2048]{1,0:T(8,128)(2,1)S(1)} fusion(bf16[32,2048]{1,0:T(8,128)(2,1)S(1)} %convolution_convert_fusion.4, bf16[2048,2048]{1,0:T(8,128)(2,1)} %param.6, f32[2048]{0:T(1024)S(1)} %get-tuple-element.5, f32[2048]{0:T(1024)S(1)} %get-tuple-element.4), kind=kOutput, calls=%fused_computation.17 | convolution fusion | flops 293666816 | bytes 8667136 | tf_op jit(solution)/shard_map/dot_general | solution.py:88
  525.0 29.0 %all_to_all.188 = bf16[8,32,2048]{2,1,0:T(8,128)(2,1)S(1)} all-to-all(bf16[8,32,2048]{2,1,0:T(8,128)(2,1)S(1)} %broadcast_in_dim.104), channel_id=1, replica_groups=mesh['samp'=8,'snp'=32] {'samp'}, dimensions={0} | all-to-all | bytes 2097152 | tf_op jit(solution)/shard_map/all_to_all | solution.py:22
  554.9 14.0 %all_to_all.189 = f32[32,1,1024]{2,1,0:T(1,128)S(1)} all-to-all(f32[32,1,1024]{2,1,0:T(1,128)S(1)} %reshape.129), channel_id=1, replica_groups=mesh['samp'=8,'snp'=32] {'snp'}, dimensions={0} | all-to-all | bytes 262144 | tf_op jit(solution)/shard_map/all_to_all | solution.py:22
  577.4 7.7 %fusion.5 = bf16[32,1,2048]{2,0,1:T(8,128)(2,1)S(1)} fusion(bf16[32,2048]{1,0:T(8,128)(2,1)S(1)} %convolution_convert_fusion.3, bf16[2048,2048]{1,0:T(8,128)(2,1)} %param.6, f32[2048]{0:T(1024)S(1)} %get-tuple-element.5, f32[2048]{0:T(1024)S(1)} %get-tuple-element.4), kind=kOutput, calls=%fused_computation.32 | convolution fusion | flops 293666816 | bytes 8667136 | tf_op jit(solution)/shard_map/dot_general | solution.py:76
  585.8 11.3 %all_to_all.190 = bf16[32,2,1024]{2,1,0:T(2,128)(2,1)S(1)} all-to-all(bf16[32,2,1024]{2,1,0:T(2,128)(2,1)S(1)} %reshape.131), channel_id=1, replica_groups=mesh['samp'=8,'snp'=32] {'snp'}, dimensions={0} | all-to-all | bytes 262144 | tf_op jit(solution)/shard_map/all_to_all | solution.py:37
  599.0 11.2 %all_to_all.191 = bf16[32,2,1024]{2,1,0:T(2,128)(2,1)S(1)} all-to-all(bf16[32,2,1024]{2,1,0:T(2,128)(2,1)S(1)} %reshape.133), channel_id=1, replica_groups=mesh['samp'=8,'snp'=32] {'snp'}, dimensions={0} | all-to-all | bytes 262144 | tf_op jit(solution)/shard_map/all_to_all | solution.py:22
  610.7 9.2 %all_to_all.192 = f32[8,1,1024]{2,1,0:T(1,128)S(1)} all-to-all(f32[8,1,1024]{2,1,0:T(1,128)S(1)} %reshape.135), channel_id=1, replica_groups=mesh['samp'=8,'snp'=32] {'samp'}, dimensions={0} | all-to-all | bytes 65536 | tf_op jit(solution)/shard_map/all_to_all | solution.py:22
  628.2 9.2 %convolution_convert_fusion.14 = bf16[32,2048]{1,0:T(8,128)(2,1)S(1)} fusion(bf16[32,2048]{1,0:T(8,128)(2,1)S(1)} %convolution_convert_fusion.2, bf16[2048,2048]{1,0:T(8,128)(2,1)} %param.6, f32[2048]{0:T(1024)S(1)} %get-tuple-element.5, f32[2048]{0:T(1024)S(1)} %get-tuple-element.4), kind=kOutput, calls=%fused_computation.15 | convolution fusion | flops 293666816 | bytes 8667136 | tf_op jit(solution)/shard_map/dot_general | solution.py:88
  637.5 29.0 %all_to_all.193 = bf16[8,32,2048]{2,1,0:T(8,128)(2,1)S(1)} all-to-all(bf16[8,32,2048]{2,1,0:T(8,128)(2,1)S(1)} %broadcast_in_dim.108), channel_id=1, replica_groups=mesh['samp'=8,'snp'=32] {'samp'}, dimensions={0} | all-to-all | bytes 2097152 | tf_op jit(solution)/shard_map/all_to_all | solution.py:22
  667.3 14.0 %all_to_all.194 = f32[32,1,1024]{2,1,0:T(1,128)S(1)} all-to-all(f32[32,1,1024]{2,1,0:T(1,128)S(1)} %reshape.137), channel_id=1, replica_groups=mesh['samp'=8,'snp'=32] {'snp'}, dimensions={0} | all-to-all | bytes 262144 | tf_op jit(solution)/shard_map/all_to_all | solution.py:22
  689.9 7.7 %fusion.6 = bf16[32,1,2048]{2,0,1:T(8,128)(2,1)S(1)} fusion(bf16[32,2048]{1,0:T(8,128)(2,1)S(1)} %convolution_convert_fusion.1, bf16[2048,2048]{1,0:T(8,128)(2,1)} %param.6, f32[2048]{0:T(1024)S(1)} %get-tuple-element.5, f32[2048]{0:T(1024)S(1)} %get-tuple-element.4), kind=kOutput, calls=%fused_computation.33 | convolution fusion | flops 293666816 | bytes 8667136 | tf_op jit(solution)/shard_map/dot_general | solution.py:76
  698.4 11.3 %all_to_all.195 = bf16[32,2,1024]{2,1,0:T(2,128)(2,1)S(1)} all-to-all(bf16[32,2,1024]{2,1,0:T(2,128)(2,1)S(1)} %reshape.139), channel_id=1, replica_groups=mesh['samp'=8,'snp'=32] {'snp'}, dimensions={0} | all-to-all | bytes 262144 | tf_op jit(solution)/shard_map/all_to_all | solution.py:37
  711.6 11.2 %all_to_all.196 = bf16[32,2,1024]{2,1,0:T(2,128)(2,1)S(1)} all-to-all(bf16[32,2,1024]{2,1,0:T(2,128)(2,1)S(1)} %reshape.141), channel_id=1, replica_groups=mesh['samp'=8,'snp'=32] {'snp'}, dimensions={0} | all-to-all | bytes 262144 | tf_op jit(solution)/shard_map/all_to_all | solution.py:22
  723.3 9.2 %all_to_all.197 = f32[8,1,1024]{2,1,0:T(1,128)S(1)} all-to-all(f32[8,1,1024]{2,1,0:T(1,128)S(1)} %reshape.143), channel_id=1, replica_groups=mesh['samp'=8,'snp'=32] {'samp'}, dimensions={0} | all-to-all | bytes 65536 | tf_op jit(solution)/shard_map/all_to_all | solution.py:22
  (279 shorter events, 132.0 us)
Async XLA Ops:
  689.9 7.7 %copy-start = (bf16[32,2048]{1,0:T(8,128)(2,1)}, bf16[32,2048]{1,0:T(8,128)(2,1)S(1)}, u32[]{:S(2)}) copy-start(bf16[32,2048]{1,0:T(8,128)(2,1)S(1)} %convolution_convert_fusion.1) | copy-start | bytes 393220
where the time goes:
time: 751 us; the launch traced here: 742 us
  blocking collectives  491 us (65%)
  matrix products  120 us (16%)
  other arithmetic  116 us (15%)
  local copies, waits for them, and re-layouts  11.5 us (2%)
    all_to_all x26, blocking collectives, from_everyone(): return lax.all_to_all(copies, axis, split_axis=0, concat_axis=0, tiled=True)  408 us
    all_to_all x7, blocking collectives, sum_at_owner(): lax.all_to_all(split_up(value, dim, length), axis, 0, 0, tiled=True)  83.6 us
    dot_general x6, matrix products, snp_side(): partial_rows = jnp.dot(qmat, xmat, preferred_element_type=jnp.float32)  55.4 us
    dot_general x7, matrix products, sample_side(): lax.dot_general(left.astype(jnp.bfloat16), xmat, (((1,), (1,)), ((), ()))...  55.1 us
    another operation x39, other arithmetic, apply_factor(): lower = jnp.linalg.cholesky(gram_total / count)  46.8 us
    another operation x26, other arithmetic, apply_factor(): return jax.scipy.linalg.solve_triangular(lower, rows, lower=True)  40.1 us

commit v1 on v0

v1 whole, which is shorter than its diff:
```python
import functools

import jax
import jax.numpy as jnp
from jax import lax
from jax.experimental import pallas as pl
from jax.experimental.pallas import tpu as pltpu
from jax.sharding import PartitionSpec as P

ITERS = 6
K = 32
LANES = 128
BLOCK = 256
EARLY = 1
MESH = pl.DeviceIdType.MESH
HIGHEST = lax.Precision.HIGHEST


def offsets(count):
    return sorted(range(count), key=lambda o: (-min(o, count - o), o))


def kernel(
    nz, ns, sample_count, snp_count,
    geno_ref, freq_ref, seed_ref, q_ref, p_ref,
    x_ref, snd_s, rcv_s, all_s, snd_z, rcv_z, all_z, gram_s, gram_z,
    load_sem, sum_s_send, sum_s_recv, all_s_send, all_s_recv,
    sum_z_send, sum_z_recv, all_z_send, all_z_recv,
    gram_s_send, gram_s_recv, gram_s_far, gram_z_send, gram_z_recv,
):
    z = lax.axis_index("samp")
    s = lax.axis_index("snp")
    chip = s // 2
    owner = lax.rem(s, 2) == 0
    rows = x_ref.shape[0]
    chips = ns // 2
    blocks_s = rows // BLOCK
    per_z = all_z.shape[0] // nz
    barrier = pltpu.get_barrier_semaphore()

    def load(block):
        part = pl.ds(pl.multiple_of(block * BLOCK, BLOCK), BLOCK)
        return pltpu.make_async_copy(geno_ref.at[part], x_ref.at[part], load_sem.at[block])

    first = chip // 2
    order_s = offsets(blocks_s)
    for off in order_s:
        load(lax.rem(first + off, blocks_s)).start()

    @pl.loop(1, ns)
    def _(d):
        pl.semaphore_signal(barrier, 1, device_id={"snp": lax.rem(s + d, ns)}, device_id_type=MESH)

    @pl.loop(1, nz)
    def _(d):
        pl.semaphore_signal(barrier, 1, device_id={"samp": lax.rem(z + d, nz)}, device_id_type=MESH)

    def send(src, dst, send_sem, recv_sem, target):
        pltpu.make_async_remote_copy(
            src_ref=src, dst_ref=dst, send_sem=send_sem, recv_sem=recv_sem,
            device_id=target, device_id_type=MESH,
        ).start()

    def settle(ref, sem):
        pltpu.make_async_copy(ref, ref, sem).wait()

    def whole(ref):
        return jnp.concatenate([ref[t] for t in range(ref.shape[0])], axis=1)

    def send_tile_s(tile):
        send(snd_s.at[tile], rcv_s.at[s], sum_s_send, sum_s_recv, {"snp": 2 * tile})

    def store_tiles(ref, block, values):
        packed = values.astype(jnp.bfloat16)
        for t in range(BLOCK // LANES):
            ref[block * (BLOCK // LANES) + t] = packed[:, t * LANES : (t + 1) * LANES]

    def product_to_samples(left, factor, prepare=None):
        pending = None
        for off in order_s:
            block = lax.rem(first + off, blocks_s)
            part = pl.ds(pl.multiple_of(block * BLOCK, BLOCK), BLOCK)
            if prepare is not None:
                prepare(block, part)
            values = lax.dot_general(
                left, x_ref[part, :], (((1,), (1,)), ((), ())), preferred_element_type=jnp.float32
            )
            if factor is not None:
                values = jnp.dot(factor, values, precision=HIGHEST, preferred_element_type=jnp.float32)
            store_tiles(snd_s, block, values)
            if pending is not None:
                send_tile_s(2 * pending)
                send_tile_s(2 * pending + 1)
            pending = block
        mate = chip + 1 - 2 * lax.rem(chip, 2)
        send_tile_s(mate)

        @pl.when(owner)
        def _():
            rcv_s[s] = snd_s[chip]

        @pl.when(jnp.logical_not(owner))
        def _():
            send_tile_s(chip)

    def sum_samples():
        settle(rcv_s.at[pl.ds(0, ns - 1)], sum_s_recv)
        total = rcv_s[0].astype(jnp.float32)
        for i in range(1, ns):
            total = total + rcv_s[i].astype(jnp.float32)
        return total

    def sent_samples():
        @pl.when(owner)
        def _():
            settle(snd_s.at[pl.ds(0, chips - 1)], sum_s_send)

        @pl.when(jnp.logical_not(owner))
        def _():
            settle(snd_s, sum_s_send)

    def share_samples(piece):
        all_s[chip] = piece.astype(jnp.bfloat16)

        @pl.loop(1, ns)
        def _(d):
            send(all_s.at[chip], all_s.at[chip], all_s_send, all_s_recv, {"snp": lax.rem(s + d, ns)})

    def await_samples():
        @pl.when(owner)
        def _():
            settle(all_s.at[pl.ds(0, chips - 1)], all_s_recv)
            settle(rcv_s.at[pl.ds(0, ns - 1)], all_s_send)

        @pl.when(jnp.logical_not(owner))
        def _():
            settle(all_s, all_s_recv)

    order_z = offsets(nz)

    def product_to_snps(left, factor):
        width = per_z * LANES
        pending = None

        def ship(block):
            part = pl.ds(block * per_z, per_z)
            send(snd_z.at[part], rcv_z.at[z], sum_z_send, sum_z_recv, {"samp": block})

        for off in order_z:
            block = lax.rem(z + off, nz)
            part = pl.ds(pl.multiple_of(block * width, width), width)
            values = jnp.dot(left, x_ref[:, part], preferred_element_type=jnp.float32)
            if factor is not None:
                values = jnp.dot(factor, values, precision=HIGHEST, preferred_element_type=jnp.float32)
            packed = values.astype(jnp.bfloat16)
            for t in range(per_z):
                tile = packed[:, t * LANES : (t + 1) * LANES]
                if off == 0:
                    rcv_z[z, t] = tile
                else:
                    snd_z[block * per_z + t] = tile
            if pending is not None:
                ship(pending)
            pending = block

    def sum_snps():
        settle(rcv_z.at[pl.ds(0, nz - 1)], sum_z_recv)
        total = rcv_z[0].astype(jnp.float32)
        for i in range(1, nz):
            total = total + rcv_z[i].astype(jnp.float32)
        return jnp.concatenate([total[t] for t in range(per_z)], axis=1)

    def share_snps(piece):
        packed = piece.astype(jnp.bfloat16)
        for t in range(per_z):
            all_z[z * per_z + t] = packed[:, t * LANES : (t + 1) * LANES]
        part = pl.ds(z * per_z, per_z)

        for off in order_z[:-1]:
            send(all_z.at[part], all_z.at[part], all_z_send, all_z_recv, {"samp": lax.rem(z + off, nz)})

    def await_snps():
        others = pl.ds(0, (nz - 1) * per_z)
        settle(all_z.at[others], all_z_recv)
        settle(all_z.at[others], all_z_send)
        settle(snd_z.at[others], sum_z_send)

    def packed_gram(left):
        four = jnp.concatenate([left] * 4, axis=0)
        wide = lax.dot_general(left, four, (((1,), (1,)), ((), ())), preferred_element_type=jnp.float32)
        band = lax.broadcasted_iota(jnp.int32, (8, LANES), 1) // K
        out = wide[0:8]
        for b in range(1, 4):
            out = jnp.where(band == b, wide[8 * b : 8 * b + 8], out)
        return out

    def send_gram_z(left):
        gram_z[z] = packed_gram(left)
        for off in order_z[:-1]:
            send(gram_z.at[z], gram_z.at[z], gram_z_send, gram_z_recv, {"samp": lax.rem(z + off, nz)})

    def take_gram_z():
        settle(gram_z.at[pl.ds(0, nz - 1)], gram_z_recv)
        settle(gram_z.at[pl.ds(0, nz - 1)], gram_z_send)
        total = gram_z[0]
        for i in range(1, nz):
            total = total + gram_z[i]
        return inverse_factor(total * (1.0 / sample_count))

    def send_gram_s(left, everyone):
        gram_s[s] = packed_gram(left)

        @pl.loop(1, chips)
        def _(d):
            send(gram_s.at[s], gram_s.at[s], gram_s_send, gram_s_recv, {"snp": 2 * lax.rem(chip + d, chips)})

        @pl.when(jnp.logical_not(owner))
        def _():
            send(gram_s.at[s], gram_s.at[s], gram_s_send, gram_s_recv, {"snp": s - 1})

        @pl.when(everyone)
        def _():
            @pl.loop(1, chips)
            def _(d):
                send(gram_s.at[s], gram_s.at[s], gram_s_far, gram_s_recv, {"snp": 2 * lax.rem(chip + d, chips) + 1})

            @pl.when(owner)
            def _():
                send(gram_s.at[s], gram_s.at[s], gram_s_far, gram_s_recv, {"snp": s + 1})

    def sent_gram_s(everyone):
        @pl.when(owner)
        def _():
            settle(gram_s.at[pl.ds(0, chips - 1)], gram_s_send)

        @pl.when(jnp.logical_not(owner))
        def _():
            settle(gram_s.at[pl.ds(0, chips)], gram_s_send)

        @pl.when(jnp.logical_and(everyone, owner))
        def _():
            settle(gram_s.at[pl.ds(0, chips)], gram_s_far)

        @pl.when(jnp.logical_and(everyone, jnp.logical_not(owner)))
        def _():
            settle(gram_s.at[pl.ds(0, chips - 1)], gram_s_far)

    def take_gram_s():
        settle(gram_s.at[pl.ds(0, ns - 1)], gram_s_recv)
        total = gram_s[0]
        for i in range(1, ns):
            total = total + gram_s[i]
        return inverse_factor(total * (1.0 / snp_count))

    def inverse_factor(packed):
        lane = lax.broadcasted_iota(jnp.int32, (K, LANES), 1)
        row = lax.broadcasted_iota(jnp.int32, (K, LANES), 0)
        bands = [pltpu.roll(packed, (K - K * b) % LANES, 1) for b in range(4)]
        mat = jnp.where(lane == row, 1.0, jnp.concatenate(bands, axis=0))
        mat = jnp.where(jnp.logical_and(lane < K, lane != row), 0.0, mat)
        for j in range(K - 1):
            line = mat[j : j + 1, :]
            column = mat[:, K + j : K + j + 1]
            share = column * (1.0 / line[:, K + j : K + j + 1])
            mat = mat - jnp.where(row > j, share, 0.0) * line
        diagonal = jnp.sum(jnp.where(lane == row + K, mat, 0.0), axis=1, keepdims=True)
        return (mat * lax.rsqrt(diagonal))[:, :K]

    def apply(factor, values):
        return jnp.dot(factor, values, precision=HIGHEST, preferred_element_type=jnp.float32)

    double = 2.0 * freq_ref[...]
    scale = lax.rsqrt(double * (1.0 - freq_ref[...]))

    def prepare(block, part):
        load(block).wait()

        @pl.loop(0, BLOCK // 32)
        def _(i):
            lines = pl.ds(pl.multiple_of(block * BLOCK + i * 32, 32), 32)
            values = x_ref[lines, :].astype(jnp.float32)
            x_ref[lines, :] = jnp.where(values < 3.0, (values - double) * scale, 0.0).astype(jnp.bfloat16)

    for off in order_s:
        block = lax.rem(first + off, blocks_s)
        prepare(block, None)
    pl.semaphore_wait(barrier, ns - 1 + nz - 1)

    def finish_samples(factor):
        @pl.when(owner)
        def _():
            total = sum_samples()
            share_samples(total if factor is None else apply(factor(), total))

        sent_samples()

    product_to_samples(seed_ref[...].astype(jnp.bfloat16), None)
    finish_samples(None)
    await_samples()

    def first_round():
        left = whole(all_s)
        send_gram_z(left)
        product_to_snps(left, take_gram_z())
        share_snps(sum_snps())
        await_snps()

    def early_samples():
        left = whole(all_z)
        send_gram_s(left, True)
        factor = take_gram_s()
        sent_gram_s(True)
        product_to_samples(left, factor)
        finish_samples(None)
        await_samples()

    def to_snps():
        left = whole(all_s)
        send_gram_z(left)
        product_to_snps(left, None)
        factor = take_gram_z()
        share_snps(apply(factor, sum_snps()))
        await_snps()

    def to_samples(last):
        left = whole(all_z)
        send_gram_s(left, last)
        product_to_samples(left, None)
        finish_samples(take_gram_s)

        @pl.when(last)
        def _():
            @pl.when(jnp.logical_not(owner))
            def _():
                settle(gram_s.at[pl.ds(0, ns - 1)], gram_s_recv)

            total = gram_s[0]
            for i in range(1, ns):
                total = total + gram_s[i]
            factor = inverse_factor(total * (1.0 / snp_count))
            p_ref[...] = apply(factor, whole(all_z).astype(jnp.float32)).astype(jnp.bfloat16)

        sent_gram_s(last)
        await_samples()

    first_round()
    if EARLY > 1:
        early_samples()
    else:
        to_samples(False)

    @pl.loop(1, ITERS)
    def _(i):
        to_snps()
        to_samples(i == ITERS - 1)

    left = whole(all_s)
    send_gram_z(left)
    q_ref[...] = apply(take_gram_z(), left.astype(jnp.float32)).astype(jnp.bfloat16)


def per_device(nz, ns, genotypes, frequency, seed_matrix):
    samples, snps = genotypes.shape
    tiles_s, tiles_z = samples // LANES, snps // LANES
    bf16, f32 = jnp.bfloat16, jnp.float32
    vmem = pl.BlockSpec(memory_space=pltpu.VMEM)
    dma = pltpu.SemaphoreType.DMA
    return pl.pallas_call(
        functools.partial(kernel, nz, ns, float(samples * nz), float(snps * ns)),
        out_shape=(
            jax.ShapeDtypeStruct((K, samples), bf16),
            jax.ShapeDtypeStruct((K, snps), bf16),
        ),
        in_specs=[pl.BlockSpec(memory_space=pl.ANY), vmem, vmem],
        out_specs=(vmem, vmem),
        scratch_shapes=[
            pltpu.VMEM((samples, snps), bf16),
            pltpu.VMEM((tiles_s, K, LANES), bf16),
            pltpu.VMEM((ns, K, LANES), bf16),
            pltpu.VMEM((tiles_s, K, LANES), bf16),
            pltpu.VMEM((tiles_z, K, LANES), bf16),
            pltpu.VMEM((nz, tiles_z // nz, K, LANES), bf16),
            pltpu.VMEM((tiles_z, K, LANES), bf16),
            pltpu.VMEM((ns, 8, LANES), f32),
            pltpu.VMEM((nz, 8, LANES), f32),
            dma((samples // BLOCK,)),
        ]
        + [dma(())] * 13,
        compiler_params=pltpu.CompilerParams(
            collective_id=0, has_side_effects=True, vmem_limit_bytes=48 * 1024 * 1024
        ),
    )(genotypes, frequency.reshape(1, snps), seed_matrix)


def solution(mesh):
    placed = (P("samp", "snp"), P("snp"), P(None, "snp"))
    return jax.shard_map(
        functools.partial(per_device, mesh.shape["samp"], mesh.shape["snp"]),
        mesh=mesh,
        in_specs=placed,
        out_specs=(P(None, "samp"), P(None, "snp")),
        check_vma=False,
    )
```

time: 751 us -> 227 us (0.30); the launches traced: 742 us -> 227 us
  blocking collectives: 491 us -> 0 us
  Pallas kernels: 0 us -> 223 us
  matrix products: 120 us -> 0 us
  other arithmetic: 116 us -> 0 us
  local copies, waits for them, and re-layouts: 11.5 us -> 2.95 us
    all_to_all x33 -> x0, blocking collectives: 491 us -> none  [the longest x26 408 us: from_everyone(): return lax.all_to_all(copies, axis, split_axis=0, concat_axis=0, tiled=True)]
    pallas_call x0 -> x1, Pallas kernels: none -> 223 us  [per_device(): pl.pallas_call(functools.partial(kernel, nz, ns, float(samples * nz), flo...]
    dot_general x26 -> x0, matrix products: 114 us -> none  [the longest x6 55.4 us: snp_side(): partial_rows = jnp.dot(qmat, xmat, preferred_element_type=jnp.float32)]
    another operation x65 -> x0, other arithmetic: 86.9 us -> none  [the longest x39 46.8 us: apply_factor(): lower = jnp.linalg.cholesky(gram_total / count)]
    all_to_all x13 -> x0, other arithmetic: 11.3 us -> none  [from_everyone(): return lax.all_to_all(copies, axis, split_axis=0, concat_axis=0, tiled=True)]
    broadcast_in_dim x7 -> x0, other arithmetic: 9.65 us -> none  [from_everyone(): copies = jnp.broadcast_to(value, (lax.axis_size(axis), *value.shape))]
where the time goes in v1:
time: 227 us
  Pallas kernels  223 us (98%)
  local copies, waits for them, and re-layouts  2.95 us (1%)
    pallas_call x1, Pallas kernels, per_device(): pl.pallas_call(functools.partial(kernel, nz, ns, float(samples * nz), flo...  223 us

profile of v1, /device:TPU:1, one launch (start us, length us, event | category | flops | bytes accessed | tf_op | source)
XLA Modules:
  0.0 226.7 jit_solution(16184927646297516)
XLA Ops:
  0.6 0.0 copy-start
  0.6 0.9 copy-done
  1.6 0.0 copy-start.1
  1.6 0.7 copy-done.1
  2.3 223.1 %shard_map.50 = (bf16[32,2048]{1,0:T(8,128)(2,1)S(1)}, bf16[32,2048]{1,0:T(8,128)(2,1)S(1)}) custom-call(bf16[2048,2048]{1,0:T(8,128)(2,1)} %geno_ref.1, f32[1,2048]{1,0:T(1,128)S(1)} %bitcast.1, f32[32,2048]{1,0:T(8,128)S(1)} %copy-done), custom_call_target="tpu_custom_call" | custom-call | tf_op jit(solution)/shard_map/pallas_call | solution.py:368
  225.4 0.7 copy.7
  226.0 0.7 copy.8
Async XLA Ops:
  0.6 1.0 copy-start
  1.6 0.7 copy-start.1

commit v2 on v1

v2 whole, which is shorter than its diff:
```python
import functools
import math

import jax
import jax.numpy as jnp
from jax import lax
from jax.experimental import pallas as pl
from jax.experimental.pallas import tpu as pltpu
from jax.sharding import PartitionSpec as P

ITERS = 6
K = 32
LANES = 128
BLOCK = 256
PANEL = 8
MESH = pl.DeviceIdType.MESH
HIGHEST = lax.Precision.HIGHEST


def hops(offset, count):
    return min(offset, count - offset)


def apply(factor, values):
    return jnp.dot(factor, values, precision=HIGHEST, preferred_element_type=jnp.float32)


def packed_gram(wide):
    band = lax.broadcasted_iota(jnp.int32, (8, LANES), 1) // K
    out = wide[0:8]
    for b in range(1, 4):
        out = jnp.where(band == b, wide[8 * b : 8 * b + 8], out)
    return out


def inverse_factor(packed):
    lane = lax.broadcasted_iota(jnp.int32, (8, LANES), 1)
    row = lax.broadcasted_iota(jnp.int32, (8, LANES), 0)
    bands = []
    for b in range(4):
        shift = (K - K * b) % LANES
        band = pltpu.roll(packed, shift, 1) if shift else packed
        bands.append(jnp.where(lane < K, jnp.where(lane == row + 8 * b, 1.0, 0.0), band))
    for p in range(K // PANEL):
        start = K + PANEL * p
        columns = [
            [jnp.broadcast_to(bands[b][:, start + c : start + c + 1], (8, LANES)) for b in range(p, 4)]
            for c in range(PANEL)
        ]
        for c in range(PANEL):
            inverse = 1.0 / columns[c][0][c : c + 1, :]
            line = bands[p][c : c + 1, :] * inverse
            heads = [columns[d][0][c : c + 1, :] * inverse for d in range(c + 1, PANEL)]
            for b in range(p, 4):
                share = columns[c][b - p]
                if b == p:
                    share = jnp.where(row > c, share, 0.0)
                bands[b] = bands[b] - share * line
                for d in range(c + 1, PANEL):
                    columns[d][b - p] = columns[d][b - p] - share * heads[d - c - 1]
    out = []
    for b in range(4):
        diagonal = jnp.sum(jnp.where(lane == row + K + 8 * b, bands[b], 0.0), axis=1, keepdims=True)
        out.append(bands[b] * lax.rsqrt(diagonal))
    return jnp.concatenate(out, axis=0)[:, :K]


def kernel(
    nz, ns, sample_count, snp_count,
    geno_ref, freq_ref, seed_ref, q_ref, p_ref,
    x_ref, acc_ref, snd_s, rcv_s, all_s, snd_z, rcv_z, all_z, gram_s, gram_z,
    load_sem, all_s_recv, all_z_recv, sum_s_send, sum_s_recv, all_s_send,
    sum_z_send, sum_z_recv, all_z_send,
    gram_s_send, gram_s_recv, gram_s_far, gram_z_send, gram_z_recv,
):
    z = lax.axis_index("samp")
    s = lax.axis_index("snp")
    chip = s // 2
    owner = lax.rem(s, 2) == 0
    rows = x_ref.shape[0]
    chips = ns // 2
    side = math.isqrt(chips)
    halves = side // 2
    x, y = chip // side, lax.rem(chip, side)
    half = y // 2
    barrier = pltpu.get_barrier_semaphore()
    per_block = BLOCK // LANES

    near_s = sorted(
        ((dx, dh) for dx in range(side) for dh in range(halves)), key=lambda o: (hops(o[0], side) + o[1], o)
    )
    near_z = sorted(range(nz), key=lambda o: (hops(o, nz), o))
    places = sorted(
        ((dx, dy, dc) for dx in range(side) for dy in range(side) for dc in range(2)),
        key=lambda o: (-hops(o[0], side) - hops(o[1], side), o),
    )

    def block_s(offset):
        return lax.rem(x + offset[0], side) * halves + lax.rem(half + offset[1], halves)

    def place_s(offset):
        return (lax.rem(x + offset[0], side) * side + lax.rem(y + offset[1], side)) * 2

    def place_z(offset):
        return lax.rem(z + offset, nz)

    def span(block):
        return pl.ds(pl.multiple_of(block * BLOCK, BLOCK), BLOCK)

    def load(block):
        return pltpu.make_async_copy(geno_ref.at[span(block)], x_ref.at[span(block)], load_sem.at[block])

    for offset in reversed(near_s):
        load(block_s(offset)).start()

    @pl.loop(1, ns)
    def _(d):
        pl.semaphore_signal(barrier, 1, device_id={"snp": lax.rem(s + d, ns)}, device_id_type=MESH)

    @pl.loop(1, nz)
    def _(d):
        pl.semaphore_signal(barrier, 1, device_id={"samp": lax.rem(z + d, nz)}, device_id_type=MESH)

    def send(src, dst, send_sem, recv_sem, target):
        pltpu.make_async_remote_copy(
            src_ref=src, dst_ref=dst, send_sem=send_sem, recv_sem=recv_sem,
            device_id=target, device_id_type=MESH,
        ).start()

    def settle(ref, sem):
        pltpu.make_async_copy(ref, ref, sem).wait()

    def two(ref, block):
        return jnp.concatenate([ref[block * per_block + t] for t in range(per_block)], axis=1)

    def whole(ref):
        return jnp.concatenate([ref[t] for t in range(ref.shape[0])], axis=1)

    def band_product(left):
        four = jnp.concatenate([left] * 4, axis=0)
        return lax.dot_general(left, four, (((1,), (1,)), ((), ())), preferred_element_type=jnp.float32)

    def times_xt(left, lines, columns):
        return lax.dot_general(
            left, x_ref[lines, columns], (((1,), (1,)), ((), ())), preferred_element_type=jnp.float32
        )

    def times_x(left, lines, columns):
        return jnp.dot(left, x_ref[lines, columns], preferred_element_type=jnp.float32)


    def send_tile_s(tile):
        send(snd_s.at[tile], rcv_s.at[s], sum_s_send, sum_s_recv, {"snp": 2 * tile})

    def ship_s(product):
        pending = None
        for offset in reversed(near_s):
            block = block_s(offset)
            packed = product(block).astype(jnp.bfloat16)
            for t in range(per_block):
                snd_s[block * per_block + t] = packed[:, t * LANES : (t + 1) * LANES]
            if pending is not None:
                for t in range(per_block):
                    send_tile_s(pending * per_block + t)
            pending = block
        send_tile_s(chip + 1 - 2 * lax.rem(chip, 2))

        @pl.when(owner)
        def _():
            rcv_s[s] = snd_s[chip]

        @pl.when(jnp.logical_not(owner))
        def _():
            send_tile_s(chip)

    def finish_samples(factor):
        @pl.when(owner)
        def _():
            inverse = None if factor is None else factor()
            settle(rcv_s.at[pl.ds(0, ns - 1)], sum_s_recv)
            total = rcv_s[0].astype(jnp.float32)
            for i in range(1, ns):
                total = total + rcv_s[i].astype(jnp.float32)
            if inverse is not None:
                total = apply(inverse, total)
            all_s[chip] = total.astype(jnp.bfloat16)
            for offset in places:
                if offset == (0, 0, 0):
                    continue
                target = {"snp": place_s(offset) + offset[2]}
                send(all_s.at[chip], all_s.at[chip], all_s_send, all_s_recv.at[chip // 2], target)
            settle(snd_s.at[pl.ds(0, chips - 1)], sum_s_send)

        @pl.when(jnp.logical_not(owner))
        def _():
            settle(snd_s, sum_s_send)

    def await_block_s(offset):
        block = block_s(offset)
        if offset == (0, 0):
            @pl.when(owner)
            def _():
                settle(all_s.at[pl.ds(0, 1)], all_s_recv.at[block])

            @pl.when(jnp.logical_not(owner))
            def _():
                settle(all_s.at[pl.ds(0, 2)], all_s_recv.at[block])
        else:
            settle(all_s.at[pl.ds(0, 2)], all_s_recv.at[block])
        return block

    def sent_all_s():
        @pl.when(owner)
        def _():
            settle(rcv_s.at[pl.ds(0, ns - 1)], all_s_send)


    def ship_z(product):
        pending = None

        def ship(block):
            part = pl.ds(block * per_block, per_block)
            send(snd_z.at[part], rcv_z.at[z], sum_z_send, sum_z_recv, {"samp": block})

        for offset in reversed(near_z):
            block = place_z(offset)
            packed = product(block).astype(jnp.bfloat16)
            for t in range(per_block):
                tile = packed[:, t * LANES : (t + 1) * LANES]
                if offset == 0:
                    rcv_z[z, t] = tile
                else:
                    snd_z[block * per_block + t] = tile
            if pending is not None:
                ship(pending)
            pending = block

    def finish_snps(inverse):
        others = pl.ds(0, (nz - 1) * per_block)
        settle(rcv_z.at[pl.ds(0, nz - 1)], sum_z_recv)
        total = rcv_z[0].astype(jnp.float32)
        for i in range(1, nz):
            total = total + rcv_z[i].astype(jnp.float32)
        total = apply(inverse, jnp.concatenate([total[t] for t in range(per_block)], axis=1))
        packed = total.astype(jnp.bfloat16)
        for t in range(per_block):
            all_z[z * per_block + t] = packed[:, t * LANES : (t + 1) * LANES]
        part = pl.ds(z * per_block, per_block)
        for offset in reversed(near_z[1:]):
            send(
                all_z.at[part], all_z.at[part], all_z_send, all_z_recv.at[nz - offset],
                {"samp": place_z(offset)},
            )
        settle(snd_z.at[others], sum_z_send)

    def await_block_z(offset):
        if offset != 0:
            settle(all_z.at[pl.ds(0, per_block)], all_z_recv.at[offset])
        return place_z(offset)

    def sent_all_z():
        settle(all_z.at[pl.ds(0, (nz - 1) * per_block)], all_z_send)


    def send_gram_z(wide):
        gram_z[z] = packed_gram(wide)
        for offset in reversed(near_z[1:]):
            send(gram_z.at[z], gram_z.at[z], gram_z_send, gram_z_recv, {"samp": place_z(offset)})

    def take_gram_z():
        settle(gram_z.at[pl.ds(0, nz - 1)], gram_z_recv)
        settle(gram_z.at[pl.ds(0, nz - 1)], gram_z_send)
        total = gram_z[0]
        for i in range(1, nz):
            total = total + gram_z[i]
        return inverse_factor(total * (1.0 / sample_count))

    def send_gram_s(wide, everyone):
        gram_s[s] = packed_gram(wide)
        for offset in places:
            if offset[2] == 0 and offset != (0, 0, 0):
                send(gram_s.at[s], gram_s.at[s], gram_s_send, gram_s_recv, {"snp": place_s(offset)})

        @pl.when(jnp.logical_not(owner))
        def _():
            send(gram_s.at[s], gram_s.at[s], gram_s_send, gram_s_recv, {"snp": s - 1})

        @pl.when(everyone)
        def _():
            @pl.loop(1, chips)
            def _(d):
                send(gram_s.at[s], gram_s.at[s], gram_s_far, gram_s_recv, {"snp": 2 * lax.rem(chip + d, chips) + 1})

            @pl.when(owner)
            def _():
                send(gram_s.at[s], gram_s.at[s], gram_s_far, gram_s_recv, {"snp": s + 1})

    def sent_gram_s(everyone):
        @pl.when(owner)
        def _():
            settle(gram_s.at[pl.ds(0, chips - 1)], gram_s_send)

        @pl.when(jnp.logical_not(owner))
        def _():
            settle(gram_s.at[pl.ds(0, chips)], gram_s_send)

        @pl.when(jnp.logical_and(everyone, owner))
        def _():
            settle(gram_s.at[pl.ds(0, chips)], gram_s_far)

        @pl.when(jnp.logical_and(everyone, jnp.logical_not(owner)))
        def _():
            settle(gram_s.at[pl.ds(0, chips - 1)], gram_s_far)

    def factor_s():
        total = gram_s[0]
        for i in range(1, ns):
            total = total + gram_s[i]
        return inverse_factor(total * (1.0 / snp_count))

    def take_gram_s():
        settle(gram_s.at[pl.ds(0, ns - 1)], gram_s_recv)
        return factor_s()

    double = 2.0 * freq_ref[...]
    scale = lax.rsqrt(double * (1.0 - freq_ref[...]))
    for offset in reversed(near_s):
        block = block_s(offset)
        load(block).wait()

        @pl.loop(0, BLOCK // 32)
        def _(i):
            lines = pl.ds(pl.multiple_of(block * BLOCK + i * 32, 32), 32)
            values = x_ref[lines, :].astype(jnp.float32)
            x_ref[lines, :] = jnp.where(values < 3.0, (values - double) * scale, 0.0).astype(jnp.bfloat16)

    pl.semaphore_wait(barrier, ns - 1 + nz - 1)
    every = slice(None)
    seed = seed_ref[...].astype(jnp.bfloat16)
    ship_s(lambda block: times_xt(seed, span(block), every))
    finish_samples(None)

    def to_snps():
        wide = None
        for i, offset in enumerate(near_s):
            block = await_block_s(offset)
            left = two(all_s, block)
            part = band_product(left)
            wide = part if wide is None else wide + part
            if i < len(near_s) - 1:
                values = times_x(left, span(block), every)
                acc_ref[...] = values if i == 0 else acc_ref[...] + values
        send_gram_z(wide)
        ship_z(lambda out: acc_ref[:, span(out)] + times_x(left, span(block), span(out)))
        sent_all_s()
        finish_snps(take_gram_z())

    def to_samples(last):
        wide = None
        for i, offset in enumerate(near_z):
            block = await_block_z(offset)
            left = two(all_z, block)
            part = band_product(left)
            wide = part if wide is None else wide + part
            if i < len(near_z) - 1:
                values = times_xt(left, every, span(block))
                acc_ref[...] = values if i == 0 else acc_ref[...] + values
        send_gram_s(wide, last)
        ship_s(lambda out: acc_ref[:, span(out)] + times_xt(left, span(out), span(block)))
        sent_all_z()
        finish_samples(take_gram_s)

        @pl.when(last)
        def _():
            @pl.when(jnp.logical_not(owner))
            def _():
                settle(gram_s.at[pl.ds(0, ns - 1)], gram_s_recv)

            p_ref[...] = apply(factor_s(), whole(all_z).astype(jnp.float32)).astype(jnp.bfloat16)

        sent_gram_s(last)

    @pl.loop(0, ITERS)
    def _(i):
        to_snps()
        to_samples(i == ITERS - 1)

    wide = None
    for offset in near_s:
        part = band_product(two(all_s, await_block_s(offset)))
        wide = part if wide is None else wide + part
    send_gram_z(wide)
    sent_all_s()
    q_ref[...] = apply(take_gram_z(), whole(all_s).astype(jnp.float32)).astype(jnp.bfloat16)


def per_device(nz, ns, genotypes, frequency, seed_matrix):
    samples, snps = genotypes.shape
    tiles_s, tiles_z = samples // LANES, snps // LANES
    bf16, f32 = jnp.bfloat16, jnp.float32
    vmem = pl.BlockSpec(memory_space=pltpu.VMEM)
    dma = pltpu.SemaphoreType.DMA
    return pl.pallas_call(
        functools.partial(kernel, nz, ns, float(samples * nz), float(snps * ns)),
        out_shape=(
            jax.ShapeDtypeStruct((K, samples), bf16),
            jax.ShapeDtypeStruct((K, snps), bf16),
        ),
        in_specs=[pl.BlockSpec(memory_space=pl.ANY), vmem, vmem],
        out_specs=(vmem, vmem),
        scratch_shapes=[
            pltpu.VMEM((samples, snps), bf16),
            pltpu.VMEM((K, max(samples, snps)), f32),
            pltpu.VMEM((tiles_s, K, LANES), bf16),
            pltpu.VMEM((ns, K, LANES), bf16),
            pltpu.VMEM((tiles_s, K, LANES), bf16),
            pltpu.VMEM((tiles_z, K, LANES), bf16),
            pltpu.VMEM((nz, tiles_z // nz, K, LANES), bf16),
            pltpu.VMEM((tiles_z, K, LANES), bf16),
            pltpu.VMEM((ns, 8, LANES), f32),
            pltpu.VMEM((nz, 8, LANES), f32),
            dma((samples // BLOCK,)),
            dma((samples // BLOCK,)),
            dma((nz,)),
        ]
        + [dma(())] * 11,
        compiler_params=pltpu.CompilerParams(
            collective_id=0, has_side_effects=True, vmem_limit_bytes=48 * 1024 * 1024
        ),
    )(genotypes, frequency.reshape(1, snps), seed_matrix)


def solution(mesh):
    placed = (P("samp", "snp"), P("snp"), P(None, "snp"))
    return jax.shard_map(
        functools.partial(per_device, mesh.shape["samp"], mesh.shape["snp"]),
        mesh=mesh,
        in_specs=placed,
        out_specs=(P(None, "samp"), P(None, "snp")),
        check_vma=False,
    )
```

time: 227 us -> 186 us (0.82)
  Pallas kernels: 223 us -> 182 us
    pallas_call x1, Pallas kernels: 223 us -> 182 us  [per_device(): pl.pallas_call(functools.partial(kernel, nz, ns, float(samples * nz), flo...]
where the time goes in v2:
time: 186 us
  Pallas kernels  182 us (98%)
  local copies, waits for them, and re-layouts  2.95 us (2%)
    pallas_call x1, Pallas kernels, per_device(): pl.pallas_call(functools.partial(kernel, nz, ns, float(samples * nz), flo...  182 us

profile of v2, /device:TPU:1, one launch (start us, length us, event | category | flops | bytes accessed | tf_op | source)
XLA Modules:
  0.0 186.0 jit_solution(8064756934790931719)
XLA Ops:
  0.6 0.0 copy-start
  0.6 0.9 copy-done
  1.6 0.0 copy-start.1
  1.6 0.7 copy-done.1
  2.3 182.4 %shard_map.50 = (bf16[32,2048]{1,0:T(8,128)(2,1)S(1)}, bf16[32,2048]{1,0:T(8,128)(2,1)S(1)}) custom-call(bf16[2048,2048]{1,0:T(8,128)(2,1)} %geno_ref.1, f32[1,2048]{1,0:T(1,128)S(1)} %bitcast.1, f32[32,2048]{1,0:T(8,128)S(1)} %copy-done), custom_call_target="tpu_custom_call" | custom-call | tf_op jit(solution)/shard_map/pallas_call | solution.py:403
  184.7 0.7 copy.7
  185.3 0.7 copy.8
Async XLA Ops:
  0.6 1.0 copy-start
  1.6 0.7 copy-start.1

commit v3 on v2

v3 whole, which is shorter than its diff:
```python
import functools
import math

import jax
import jax.numpy as jnp
from jax import lax
from jax.experimental import pallas as pl
from jax.experimental.pallas import tpu as pltpu
from jax.sharding import PartitionSpec as P

ITERS = 6
K = 32
LANES = 128
BLOCK = 256
PANEL = 8
MESH = pl.DeviceIdType.MESH
HALF = K // 2


def hops(offset, count):
    return min(offset, count - offset)


def in_parts(factor):
    high = factor.astype(jnp.bfloat16)
    rest = factor - high.astype(jnp.float32)
    middle = rest.astype(jnp.bfloat16)
    low = (rest - middle.astype(jnp.float32)).astype(jnp.bfloat16)
    return jnp.concatenate([high, middle, low], axis=0)


def apply(parts, values):
    three = jnp.dot(parts, values, preferred_element_type=jnp.float32)
    return (three[:K] + three[K : 2 * K] + three[2 * K :]).astype(jnp.bfloat16)


def packed_gram(wide):
    band = lax.broadcasted_iota(jnp.int32, (8, LANES), 1) // K
    out = wide[0:8]
    for b in range(1, 4):
        out = jnp.where(band == b, wide[8 * b : 8 * b + 8], out)
    return out


def inverse_factor(packed):
    lane = lax.broadcasted_iota(jnp.int32, (8, LANES), 1)
    row = lax.broadcasted_iota(jnp.int32, (8, LANES), 0)
    bands = []
    for b in range(4):
        shift = (K - K * b) % LANES
        band = pltpu.roll(packed, shift, 1) if shift else packed
        bands.append(jnp.where(lane < K, jnp.where(lane == row + 8 * b, 1.0, 0.0), band))
    for p in range(K // PANEL):
        start = K + PANEL * p
        columns = [
            [jnp.broadcast_to(bands[b][:, start + c : start + c + 1], (8, LANES)) for b in range(p, 4)]
            for c in range(PANEL)
        ]
        for c in range(PANEL):
            inverse = 1.0 / columns[c][0][c : c + 1, :]
            line = bands[p][c : c + 1, :] * inverse
            heads = [columns[d][0][c : c + 1, :] * inverse for d in range(c + 1, PANEL)]
            for b in range(p, 4):
                share = columns[c][b - p]
                if b == p:
                    share = jnp.where(row > c, share, 0.0)
                bands[b] = bands[b] - share * line
                for d in range(c + 1, PANEL):
                    columns[d][b - p] = columns[d][b - p] - share * heads[d - c - 1]
    out = []
    for b in range(4):
        diagonal = jnp.sum(jnp.where(lane == row + K + 8 * b, bands[b], 0.0), axis=1, keepdims=True)
        out.append(bands[b] * lax.rsqrt(diagonal))
    return jnp.concatenate(out, axis=0)[:, :K]


def kernel(
    nz, ns, sample_count, snp_count,
    geno_ref, freq_ref, seed_ref, q_ref, p_ref,
    x_ref, acc_ref, factor_ref, frequency_ref, start_ref,
    snd_s, rcv_s, all_s, snd_z, rcv_z, all_z, gram_s, gram_z, mine_ref, mate_ref,
    load_sem, all_s_recv, all_z_recv, gram_s_recv, gram_z_recv, mate_recv,
    freq_sem, seed_sem, sum_s_send, sum_s_recv, all_s_send,
    sum_z_send, sum_z_recv, all_z_send, gram_s_send, gram_z_send, mate_send,
):
    z = lax.axis_index("samp")
    s = lax.axis_index("snp")
    chip, core = s // 2, lax.rem(s, 2)
    chips = ns // 2
    side = math.isqrt(chips)
    halves = side // 2
    x, y = chip // side, lax.rem(chip, side)
    half = y // 2
    barrier = pltpu.get_barrier_semaphore()
    per_block = BLOCK // LANES
    owners = 2 * per_block
    every = slice(None)

    near_s = sorted(
        ((dx, dh) for dx in range(side) for dh in range(halves)), key=lambda o: (hops(o[0], side) + o[1], o)
    )
    near_z = sorted(range(nz), key=lambda o: (hops(o, nz), o))
    places = sorted(
        ((dx, dy, dc) for dx in range(side) for dy in range(side) for dc in range(2)),
        key=lambda o: (-hops(o[0], side) - hops(o[1], side), o),
    )
    places.remove((0, 0, 0))

    def block_s(offset):
        return lax.rem(x + offset[0], side) * halves + lax.rem(half + offset[1], halves)

    def chip_s(offset):
        return lax.rem(x + offset[0], side) * side + lax.rem(y + offset[1], side)

    def place_s(offset):
        return chip_s(offset) * 2 + lax.rem(core + offset[2], 2)

    def place_z(offset):
        return lax.rem(z + offset, nz)

    def span(block):
        return pl.ds(pl.multiple_of(block * BLOCK, BLOCK), BLOCK)

    def load(block):
        return pltpu.make_async_copy(geno_ref.at[span(block)], x_ref.at[span(block)], load_sem.at[block])

    load_freq = pltpu.make_async_copy(freq_ref, frequency_ref, freq_sem)
    load_seed = pltpu.make_async_copy(seed_ref, start_ref, seed_sem)
    load_freq.start()
    for offset in reversed(near_s):
        load(block_s(offset)).start()
    load_seed.start()

    @pl.loop(1, ns)
    def _(d):
        pl.semaphore_signal(barrier, 1, device_id={"snp": lax.rem(s + d, ns)}, device_id_type=MESH)

    @pl.loop(1, nz)
    def _(d):
        pl.semaphore_signal(barrier, 1, device_id={"samp": lax.rem(z + d, nz)}, device_id_type=MESH)

    def send(src, dst, send_sem, recv_sem, target):
        pltpu.make_async_remote_copy(
            src_ref=src, dst_ref=dst, send_sem=send_sem, recv_sem=recv_sem,
            device_id=target, device_id_type=MESH,
        ).start()

    def settle(ref, sem):
        pltpu.make_async_copy(ref, ref, sem).wait()

    def band_product(left):
        four = jnp.concatenate([left] * 4, axis=0)
        return lax.dot_general(left, four, (((1,), (1,)), ((), ())), preferred_element_type=jnp.float32)

    def times_xt(left, lines, columns):
        return lax.dot_general(
            left, x_ref[lines, columns], (((1,), (1,)), ((), ())), preferred_element_type=jnp.float32
        )

    def times_x(left, lines, columns):
        return jnp.dot(left, x_ref[lines, columns], preferred_element_type=jnp.float32)


    others_s = pl.ds(0, ns - 1)

    def ship_s(product):
        pending = None
        for offset in reversed(near_s):
            block = block_s(offset)
            packed = product(block).astype(jnp.bfloat16)
            for t in range(owners):
                column = (t // 2) * LANES
                snd_s[block * owners + t] = packed[HALF * (t % 2) : HALF * (t % 2 + 1), column : column + LANES]
            if pending is not None:
                for t in range(owners):
                    tile = pending * owners + t
                    send(snd_s.at[tile], rcv_s.at[s], sum_s_send, sum_s_recv, {"snp": tile})
            pending = block
        for t in range(1, owners):
            tile = pending * owners + lax.rem(lax.rem(s, owners) + t, owners)
            send(snd_s.at[tile], rcv_s.at[s], sum_s_send, sum_s_recv, {"snp": tile})
        rcv_s[s] = snd_s[s]

    def finish_samples():
        settle(rcv_s.at[others_s], sum_s_recv)
        total = rcv_s[0].astype(jnp.float32)
        for i in range(1, ns):
            total = total + rcv_s[i].astype(jnp.float32)
        all_s[s] = total.astype(jnp.bfloat16)
        for offset in places:
            send(all_s.at[s], all_s.at[s], all_s_send, all_s_recv.at[chip // 2], {"snp": place_s(offset)})
        settle(snd_s.at[others_s], sum_s_send)

    def take_block_s(offset):
        block = block_s(offset)
        settle(all_s.at[pl.ds(0, owners - (offset == (0, 0)))], all_s_recv.at[block])
        columns = [
            jnp.concatenate([all_s[block * owners + 2 * t], all_s[block * owners + 2 * t + 1]], axis=0)
            for t in range(per_block)
        ]
        values = apply(factor_ref[...], jnp.concatenate(columns, axis=1))
        q_ref[:, span(block)] = values
        return block, values


    others_z = pl.ds(0, nz - 1)
    other_tiles_z = pl.ds(0, (nz - 1) * per_block)

    def ship_z(product):
        pending = None

        def ship(block):
            part = pl.ds(block * per_block, per_block)
            send(snd_z.at[part], rcv_z.at[z], sum_z_send, sum_z_recv, {"samp": block})

        for offset in reversed(near_z):
            block = place_z(offset)
            packed = product(block).astype(jnp.bfloat16)
            for t in range(per_block):
                tile = packed[:, t * LANES : (t + 1) * LANES]
                if offset == 0:
                    rcv_z[z, t] = tile
                else:
                    snd_z[block * per_block + t] = tile
            if pending is not None:
                ship(pending)
            pending = block

    def finish_snps():
        settle(rcv_z.at[others_z], sum_z_recv)
        total = rcv_z[0].astype(jnp.float32)
        for i in range(1, nz):
            total = total + rcv_z[i].astype(jnp.float32)
        part = pl.ds(z * per_block, per_block)
        all_z[part] = total.astype(jnp.bfloat16)
        for offset in reversed(near_z[1:]):
            send(
                all_z.at[part], all_z.at[part], all_z_send, all_z_recv.at[nz - offset],
                {"samp": place_z(offset)},
            )
        settle(snd_z.at[other_tiles_z], sum_z_send)

    def take_block_z(offset):
        block = place_z(offset)
        if offset != 0:
            settle(all_z.at[pl.ds(0, per_block)], all_z_recv.at[offset])
        tiles = [all_z[block * per_block + t] for t in range(per_block)]
        values = apply(factor_ref[...], jnp.concatenate(tiles, axis=1))
        p_ref[:, span(block)] = values
        return block, values


    def send_gram_z(turn, wide):
        gram_z[turn, z] = packed_gram(wide)
        for offset in reversed(near_z[1:]):
            mine = gram_z.at[turn, z]
            send(mine, mine, gram_z_send, gram_z_recv.at[turn], {"samp": place_z(offset)})

    def take_gram_z(turn):
        settle(gram_z.at[turn, others_z], gram_z_recv.at[turn])
        settle(gram_z.at[turn, others_z], gram_z_send)
        total = gram_z[turn, 0]
        for i in range(1, nz):
            total = total + gram_z[turn, i]
        factor_ref[...] = in_parts(inverse_factor(total * (1.0 / sample_count)))

    other_chips = pl.ds(0, chips - 1)

    def send_gram_s(turn, wide):
        gram_s[turn, chip] = packed_gram(wide)
        for offset in places:
            if offset[2] == 0:
                mine = gram_s.at[turn, chip]
                send(mine, mine, gram_s_send, gram_s_recv.at[turn], {"snp": place_s(offset)})

    def take_gram_s(turn):
        settle(gram_s.at[turn, other_chips], gram_s_recv.at[turn])
        total = gram_s[turn, 0]
        for i in range(1, chips):
            total = total + gram_s[turn, i]
        mine_ref[...] = total
        send(mine_ref, mate_ref.at[turn], mate_send, mate_recv.at[turn], {"snp": s + 1 - 2 * core})
        settle(gram_s.at[turn, other_chips], gram_s_send)
        settle(mate_ref.at[turn], mate_recv.at[turn])
        settle(mine_ref, mate_send)
        total = (total + mate_ref[turn]) * (1.0 / snp_count)
        factor_ref[...] = in_parts(inverse_factor(total))

    load_freq.wait()
    double = 2.0 * frequency_ref[...]
    scale = lax.rsqrt(double * (1.0 - frequency_ref[...]))
    levels = [((dosage - double) * scale).astype(jnp.bfloat16) for dosage in (0.0, 1.0, 2.0)]
    eye = lax.broadcasted_iota(jnp.int32, (K, K), 0) == lax.broadcasted_iota(jnp.int32, (K, K), 1)
    factor_ref[...] = in_parts(jnp.where(eye, 1.0, 0.0))

    for offset in reversed(near_s):
        block = block_s(offset)
        load(block).wait()

        @pl.loop(0, BLOCK // 32)
        def _(i):
            lines = pl.ds(pl.multiple_of(block * BLOCK + i * 32, 32), 32)
            values = x_ref[lines, :]
            known = jnp.where(
                values == 0.0, levels[0], jnp.where(values == 1.0, levels[1], levels[2])
            )
            x_ref[lines, :] = jnp.where(values < 3.0, known, jnp.bfloat16(0.0))

    load_seed.wait()
    seed = start_ref[...].astype(jnp.bfloat16)
    pl.semaphore_wait(barrier, ns - 1 + nz - 1)
    ship_s(lambda block: times_xt(seed, span(block), every))
    finish_samples()

    def to_snps(turn):
        wide = None
        for i, offset in enumerate(near_s):
            block, left = take_block_s(offset)
            part = band_product(left)
            wide = part if wide is None else wide + part
            if i < len(near_s) - 1:
                values = times_x(left, span(block), every)
                acc_ref[...] = values if i == 0 else acc_ref[...] + values
        ship_z(lambda out: acc_ref[:, span(out)] + times_x(left, span(block), span(out)))
        send_gram_z(turn, wide)
        settle(rcv_s.at[others_s], all_s_send)
        finish_snps()
        take_gram_z(turn)

    def to_samples(turn):
        wide = None
        for i, offset in enumerate(near_z):
            block, left = take_block_z(offset)
            part = band_product(left)
            wide = part if wide is None else wide + part
            if i < len(near_z) - 1:
                values = times_xt(left, every, span(block))
                acc_ref[...] = values if i == 0 else acc_ref[...] + values
        ship_s(lambda out: acc_ref[:, span(out)] + times_xt(left, span(out), span(block)))
        send_gram_s(turn, wide)
        settle(all_z.at[other_tiles_z], all_z_send)
        finish_samples()
        take_gram_s(turn)

    @pl.loop(0, ITERS)
    def _(i):
        turn = lax.rem(i, 2)
        to_snps(turn)
        to_samples(turn)

    final = ITERS % 2
    for block in range(p_ref.shape[1] // BLOCK):
        columns = slice(block * BLOCK, (block + 1) * BLOCK)
        p_ref[:, columns] = apply(factor_ref[...], p_ref[:, columns])
    wide = None
    for offset in near_s:
        part = band_product(take_block_s(offset)[1])
        wide = part if wide is None else wide + part
    send_gram_z(final, wide)
    settle(rcv_s.at[others_s], all_s_send)
    take_gram_z(final)
    for block in range(q_ref.shape[1] // BLOCK):
        columns = slice(block * BLOCK, (block + 1) * BLOCK)
        q_ref[:, columns] = apply(factor_ref[...], q_ref[:, columns])


def per_device(nz, ns, genotypes, frequency, seed_matrix):
    samples, snps = genotypes.shape
    tiles_s, tiles_z, chips = samples // LANES, snps // LANES, ns // 2
    bf16, f32 = jnp.bfloat16, jnp.float32
    vmem, hbm = pl.BlockSpec(memory_space=pltpu.VMEM), pl.BlockSpec(memory_space=pl.ANY)
    dma = pltpu.SemaphoreType.DMA
    return pl.pallas_call(
        functools.partial(kernel, nz, ns, float(samples * nz), float(snps * ns)),
        out_shape=(
            jax.ShapeDtypeStruct((K, samples), bf16),
            jax.ShapeDtypeStruct((K, snps), bf16),
        ),
        in_specs=[hbm, hbm, hbm],
        out_specs=(vmem, vmem),
        scratch_shapes=[
            pltpu.VMEM((samples, snps), bf16),
            pltpu.VMEM((K, max(samples, snps)), f32),
            pltpu.VMEM((3 * K, K), bf16),
            pltpu.VMEM((1, snps), f32),
            pltpu.VMEM((K, snps), f32),
            pltpu.VMEM((ns, HALF, LANES), bf16),
            pltpu.VMEM((ns, HALF, LANES), bf16),
            pltpu.VMEM((ns, HALF, LANES), bf16),
            pltpu.VMEM((tiles_z, K, LANES), bf16),
            pltpu.VMEM((nz, tiles_z // nz, K, LANES), bf16),
            pltpu.VMEM((tiles_z, K, LANES), bf16),
            pltpu.VMEM((2, chips, 8, LANES), f32),
            pltpu.VMEM((2, nz, 8, LANES), f32),
            pltpu.VMEM((8, LANES), f32),
            pltpu.VMEM((2, 8, LANES), f32),
            dma((samples // BLOCK,)),
            dma((samples // BLOCK,)),
            dma((nz,)),
            dma((2,)),
            dma((2,)),
            dma((2,)),
        ]
        + [dma(())] * 11,
        compiler_params=pltpu.CompilerParams(
            collective_id=0, has_side_effects=True, vmem_limit_bytes=48 * 1024 * 1024
        ),
    )(genotypes, frequency.reshape(1, snps), seed_matrix)


def solution(mesh):
    placed = (P("samp", "snp"), P("snp"), P(None, "snp"))
    return jax.shard_map(
        functools.partial(per_device, mesh.shape["samp"], mesh.shape["snp"]),
        mesh=mesh,
        in_specs=placed,
        out_specs=(P(None, "samp"), P(None, "snp")),
        check_vma=False,
    )
```

time: 186 us -> 186 us (level)
  no operation moved by 1% of the time
where the time goes in v3:
time: 186 us; the launch traced here: 185 us
  Pallas kernels  182 us (98%)
  local copies, waits for them, and re-layouts  2.95 us (2%)
    pallas_call x1, Pallas kernels, per_device(): pl.pallas_call(functools.partial(kernel, nz, ns, float(samples * nz), flo...  182 us

profile of v3, /device:TPU:1, one launch (start us, length us, event | category | flops | bytes accessed | tf_op | source)
XLA Modules:
  0.0 185.4 jit_solution(6518467529133558854)
XLA Ops:
  0.6 0.0 copy-start
  0.6 0.9 copy-done
  1.6 0.0 copy-start.1
  1.6 0.7 copy-done.1
  2.3 181.8 %shard_map.50 = (bf16[32,2048]{1,0:T(8,128)(2,1)S(1)}, bf16[32,2048]{1,0:T(8,128)(2,1)S(1)}) custom-call(bf16[2048,2048]{1,0:T(8,128)(2,1)} %geno_ref.1, f32[1,2048]{1,0:T(1,128)S(1)} %bitcast.1, f32[32,2048]{1,0:T(8,128)S(1)} %copy-done), custom_call_target="tpu_custom_call" | custom-call | tf_op jit(solution)/shard_map/pallas_call | solution.py:373
  184.1 0.7 copy.7
  184.7 0.7 copy.8
Async XLA Ops:
  0.6 1.0 copy-start
  1.6 0.7 copy-start.1

commit v4 on v3

--- a/solution.py
+++ b/solution.py
@@ -13,6 +13,7 @@
 LANES = 128
 BLOCK = 256
 PANEL = 8
+EARLY = 5
 MESH = pl.DeviceIdType.MESH
 HALF = K // 2
 
@@ -77,7 +78,7 @@
 def kernel(
     nz, ns, sample_count, snp_count,
     geno_ref, freq_ref, seed_ref, q_ref, p_ref,
-    x_ref, acc_ref, factor_ref, frequency_ref, start_ref,
+    x_ref, xt_ref, acc_ref, factor_ref, frequency_ref, start_ref,
     snd_s, rcv_s, all_s, snd_z, rcv_z, all_z, gram_s, gram_z, mine_ref, mate_ref,
     load_sem, all_s_recv, all_z_recv, gram_s_recv, gram_z_recv, mate_recv,
     freq_sem, seed_sem, sum_s_send, sum_s_recv, all_s_send,
@@ -95,6 +96,7 @@
     per_block = BLOCK // LANES
     owners = 2 * per_block
     every = slice(None)
+    blocks_x = x_ref.shape[0] // BLOCK
 
     near_s = sorted(
         ((dx, dh) for dx in range(side) for dh in range(halves)), key=lambda o: (hops(o[0], side) + o[1], o)
@@ -105,6 +107,7 @@
         key=lambda o: (-hops(o[0], side) - hops(o[1], side), o),
     )
     places.remove((0, 0, 0))
+    early_s, early_z = max(1, len(near_s) * EARLY // 8), max(1, nz * EARLY // 8)
 
     def block_s(offset):
         return lax.rem(x + offset[0], side) * halves + lax.rem(half + offset[1], halves)
@@ -152,13 +155,19 @@
         four = jnp.concatenate([left] * 4, axis=0)
         return lax.dot_general(left, four, (((1,), (1,)), ((), ())), preferred_element_type=jnp.float32)
 
-    def times_xt(left, lines, columns):
-        return lax.dot_general(
-            left, x_ref[lines, columns], (((1,), (1,)), ((), ())), preferred_element_type=jnp.float32
-        )
-
-    def times_x(left, lines, columns):
-        return jnp.dot(left, x_ref[lines, columns], preferred_element_type=jnp.float32)
+    def product(ref, parts, columns):
+        total = None
+        for block, left in parts:
+            part = jnp.dot(left, ref[span(block), columns], preferred_element_type=jnp.float32)
+            total = part if total is None else total + part
+        return total
+
+    def transpose(first, last):
+        @pl.loop(first, last)
+        def _(i):
+            @pl.loop(0, x_ref.shape[1] // BLOCK)
+            def _(j):
+                xt_ref[span(j), span(i)] = x_ref[span(i), span(j)].T
 
 
     others_s = pl.ds(0, ns - 1)
@@ -191,16 +200,22 @@
             send(all_s.at[s], all_s.at[s], all_s_send, all_s_recv.at[chip // 2], {"snp": place_s(offset)})
         settle(snd_s.at[others_s], sum_s_send)
 
-    def take_block_s(offset):
-        block = block_s(offset)
-        settle(all_s.at[pl.ds(0, owners - (offset == (0, 0)))], all_s_recv.at[block])
-        columns = [
-            jnp.concatenate([all_s[block * owners + 2 * t], all_s[block * owners + 2 * t + 1]], axis=0)
-            for t in range(per_block)
-        ]
+    def normalized(blocks, columns, out_ref):
         values = apply(factor_ref[...], jnp.concatenate(columns, axis=1))
-        q_ref[:, span(block)] = values
-        return block, values
+        parts = [(block, values[:, i * BLOCK : (i + 1) * BLOCK]) for i, block in enumerate(blocks)]
+        for block, part in parts:
+            out_ref[:, span(block)] = part
+        return parts
+
+    def take_s(offsets):
+        blocks, columns = [], []
+        for offset in offsets:
+            block = block_s(offset)
+            settle(all_s.at[pl.ds(0, owners - (offset == (0, 0)))], all_s_recv.at[block])
+            for t in range(0, owners, 2):
+                columns.append(jnp.concatenate([all_s[block * owners + t], all_s[block * owners + t + 1]], axis=0))
+            blocks.append(block)
+        return normalized(blocks, columns, q_ref)
 
 
     others_z = pl.ds(0, nz - 1)
@@ -240,14 +255,15 @@
             )
         settle(snd_z.at[other_tiles_z], sum_z_send)
 
-    def take_block_z(offset):
-        block = place_z(offset)
-        if offset != 0:
-            settle(all_z.at[pl.ds(0, per_block)], all_z_recv.at[offset])
-        tiles = [all_z[block * per_block + t] for t in range(per_block)]
-        values = apply(factor_ref[...], jnp.concatenate(tiles, axis=1))
-        p_ref[:, span(block)] = values
-        return block, values
+    def take_z(offsets):
+        blocks, columns = [], []
+        for offset in offsets:
+            block = place_z(offset)
+            if offset != 0:
+                settle(all_z.at[pl.ds(0, per_block)], all_z_recv.at[offset])
+            columns += [all_z[block * per_block + t] for t in range(per_block)]
+            blocks.append(block)
+        return normalized(blocks, columns, p_ref)
 
 
     def send_gram_z(turn, wide):
@@ -309,35 +325,29 @@
     load_seed.wait()
     seed = start_ref[...].astype(jnp.bfloat16)
     pl.semaphore_wait(barrier, ns - 1 + nz - 1)
-    ship_s(lambda block: times_xt(seed, span(block), every))
+    ship_s(
+        lambda block: lax.dot_general(
+            seed, x_ref[span(block), :], (((1,), (1,)), ((), ())), preferred_element_type=jnp.float32
+        )
+    )
+    transpose(0, blocks_x // 2)
     finish_samples()
+    transpose(blocks_x // 2, blocks_x)
 
     def to_snps(turn):
-        wide = None
-        for i, offset in enumerate(near_s):
-            block, left = take_block_s(offset)
-            part = band_product(left)
-            wide = part if wide is None else wide + part
-            if i < len(near_s) - 1:
-                values = times_x(left, span(block), every)
-                acc_ref[...] = values if i == 0 else acc_ref[...] + values
-        ship_z(lambda out: acc_ref[:, span(out)] + times_x(left, span(block), span(out)))
-        send_gram_z(turn, wide)
+        acc_ref[...] = product(x_ref, take_s(near_s[:early_s]), every)
+        late = take_s(near_s[early_s:])
+        ship_z(lambda out: acc_ref[:, span(out)] + product(x_ref, late, span(out)))
+        send_gram_z(turn, band_product(q_ref[...]))
         settle(rcv_s.at[others_s], all_s_send)
         finish_snps()
         take_gram_z(turn)
 
     def to_samples(turn):
-        wide = None
-        for i, offset in enumerate(near_z):
-            block, left = take_block_z(offset)
-            part = band_product(left)
-            wide = part if wide is None else wide + part
-            if i < len(near_z) - 1:
-                values = times_xt(left, every, span(block))
-                acc_ref[...] = values if i == 0 else acc_ref[...] + values
-        ship_s(lambda out: acc_ref[:, span(out)] + times_xt(left, span(out), span(block)))
-        send_gram_s(turn, wide)
+        acc_ref[...] = product(xt_ref, take_z(near_z[:early_z]), every)
+        late = take_z(near_z[early_z:])
+        ship_s(lambda out: acc_ref[:, span(out)] + product(xt_ref, late, span(out)))
+        send_gram_s(turn, band_product(p_ref[...]))
         settle(all_z.at[other_tiles_z], all_z_send)
         finish_samples()
         take_gram_s(turn)
@@ -352,11 +362,8 @@
     for block in range(p_ref.shape[1] // BLOCK):
         columns = slice(block * BLOCK, (block + 1) * BLOCK)
         p_ref[:, columns] = apply(factor_ref[...], p_ref[:, columns])
-    wide = None
-    for offset in near_s:
-        part = band_product(take_block_s(offset)[1])
-        wide = part if wide is None else wide + part
-    send_gram_z(final, wide)
+    take_s(near_s)
+    send_gram_z(final, band_product(q_ref[...]))
     settle(rcv_s.at[others_s], all_s_send)
     take_gram_z(final)
     for block in range(q_ref.shape[1] // BLOCK):
@@ -380,6 +387,7 @@
         out_specs=(vmem, vmem),
         scratch_shapes=[
             pltpu.VMEM((samples, snps), bf16),
+            pltpu.VMEM((snps, samples), bf16),
             pltpu.VMEM((K, max(samples, snps)), f32),
             pltpu.VMEM((3 * K, K), bf16),
             pltpu.VMEM((1, snps), f32),

time: 186 us -> 178 us (0.957)
  Pallas kernels: 182 us -> 175 us
    pallas_call x1, Pallas kernels: 182 us -> 175 us  [per_device(): pl.pallas_call(functools.partial(kernel, nz, ns, float(samples * nz), flo...]
where the time goes in v4:
time: 178 us
  Pallas kernels  175 us (98%)
  local copies, waits for them, and re-layouts  2.95 us (2%)
    pallas_call x1, Pallas kernels, per_device(): pl.pallas_call(functools.partial(kernel, nz, ns, float(samples * nz), flo...  175 us

profile of v4, /device:TPU:1, one launch (start us, length us, event | category | flops | bytes accessed | tf_op | source)
XLA Modules:
  0.0 178.3 jit_solution(15545437490101251405)
XLA Ops:
  0.6 0.0 copy-start
  0.6 0.9 copy-done
  1.6 0.0 copy-start.1
  1.6 0.7 copy-done.1
  2.3 174.7 %shard_map.50 = (bf16[32,2048]{1,0:T(8,128)(2,1)S(1)}, bf16[32,2048]{1,0:T(8,128)(2,1)S(1)}) custom-call(bf16[2048,2048]{1,0:T(8,128)(2,1)} %geno_ref.1, f32[1,2048]{1,0:T(1,128)S(1)} %bitcast.1, f32[32,2048]{1,0:T(8,128)S(1)} %copy-done), custom_call_target="tpu_custom_call" | custom-call | tf_op jit(solution)/shard_map/pallas_call | solution.py:380
  176.9 0.7 copy.7
  177.6 0.7 copy.8
Async XLA Ops:
  0.6 1.0 copy-start
  1.6 0.7 copy-start.1

commit v5 on v4

--- a/solution.py
+++ b/solution.py
@@ -13,7 +13,8 @@
 LANES = 128
 BLOCK = 256
 PANEL = 8
-EARLY = 5
+GROUPS_S = (4, 3, 1)
+GROUPS_Z = (3, 2, 3)
 MESH = pl.DeviceIdType.MESH
 HALF = K // 2
 
@@ -107,7 +108,6 @@
         key=lambda o: (-hops(o[0], side) - hops(o[1], side), o),
     )
     places.remove((0, 0, 0))
-    early_s, early_z = max(1, len(near_s) * EARLY // 8), max(1, nz * EARLY // 8)
 
     def block_s(offset):
         return lax.rem(x + offset[0], side) * halves + lax.rem(half + offset[1], halves)
@@ -130,9 +130,9 @@
     load_freq = pltpu.make_async_copy(freq_ref, frequency_ref, freq_sem)
     load_seed = pltpu.make_async_copy(seed_ref, start_ref, seed_sem)
     load_freq.start()
+    load_seed.start()
     for offset in reversed(near_s):
         load(block_s(offset)).start()
-    load_seed.start()
 
     @pl.loop(1, ns)
     def _(d):
@@ -161,6 +161,19 @@
             part = jnp.dot(left, ref[span(block), columns], preferred_element_type=jnp.float32)
             total = part if total is None else total + part
         return total
+
+    def early_products(ref, take, near, sizes):
+        groups, start = [], 0
+        for size in sizes:
+            groups.append(near[start : start + size])
+            start += size
+        groups = [group for group in groups[:-1] if group] + [near[start - sizes[-1] :]]
+        if len(near) < start:
+            groups = [near[:1], near[1:]]
+        for i, group in enumerate(groups[:-1]):
+            values = product(ref, take(group), every)
+            acc_ref[...] = values if i == 0 else acc_ref[...] + values
+        return take(groups[-1])
 
     def transpose(first, last):
         @pl.loop(first, last)
@@ -309,8 +322,11 @@
     eye = lax.broadcasted_iota(jnp.int32, (K, K), 0) == lax.broadcasted_iota(jnp.int32, (K, K), 1)
     factor_ref[...] = in_parts(jnp.where(eye, 1.0, 0.0))
 
-    for offset in reversed(near_s):
-        block = block_s(offset)
+    load_seed.wait()
+    seed = start_ref[...].astype(jnp.bfloat16)
+    pl.semaphore_wait(barrier, ns - 1 + nz - 1)
+
+    def first_product(block):
         load(block).wait()
 
         @pl.loop(0, BLOCK // 32)
@@ -322,21 +338,17 @@
             )
             x_ref[lines, :] = jnp.where(values < 3.0, known, jnp.bfloat16(0.0))
 
-    load_seed.wait()
-    seed = start_ref[...].astype(jnp.bfloat16)
-    pl.semaphore_wait(barrier, ns - 1 + nz - 1)
-    ship_s(
-        lambda block: lax.dot_general(
+        return lax.dot_general(
             seed, x_ref[span(block), :], (((1,), (1,)), ((), ())), preferred_element_type=jnp.float32
         )
-    )
+
+    ship_s(first_product)
     transpose(0, blocks_x // 2)
     finish_samples()
     transpose(blocks_x // 2, blocks_x)
 
     def to_snps(turn):
-        acc_ref[...] = product(x_ref, take_s(near_s[:early_s]), every)
-        late = take_s(near_s[early_s:])
+        late = early_products(x_ref, take_s, near_s, GROUPS_S)
         ship_z(lambda out: acc_ref[:, span(out)] + product(x_ref, late, span(out)))
         send_gram_z(turn, band_product(q_ref[...]))
         settle(rcv_s.at[others_s], all_s_send)
@@ -344,8 +356,7 @@
         take_gram_z(turn)
 
     def to_samples(turn):
-        acc_ref[...] = product(xt_ref, take_z(near_z[:early_z]), every)
-        late = take_z(near_z[early_z:])
+        late = early_products(xt_ref, take_z, near_z, GROUPS_Z)
         ship_s(lambda out: acc_ref[:, span(out)] + product(xt_ref, late, span(out)))
         send_gram_s(turn, band_product(p_ref[...]))
         settle(all_z.at[other_tiles_z], all_z_send)

time: 178 us -> 181 us (1.017)
  Pallas kernels: 175 us -> 177 us
    pallas_call x1, Pallas kernels: 175 us -> 177 us  [per_device(): pl.pallas_call(functools.partial(kernel, nz, ns, float(samples * nz), flo...]
where the time goes in v5:
time: 181 us
  Pallas kernels  177 us (98%)
  local copies, waits for them, and re-layouts  2.95 us (2%)
    pallas_call x1, Pallas kernels, per_device(): pl.pallas_call(functools.partial(kernel, nz, ns, float(samples * nz), flo...  177 us

profile of v5, /device:TPU:1, one launch (start us, length us, event | category | flops | bytes accessed | tf_op | source)
XLA Modules:
  0.0 181.0 jit_solution(2976118156990649779)
XLA Ops:
  0.6 0.0 copy-start
  0.6 0.9 copy-done
  1.6 0.0 copy-start.1
  1.6 0.7 copy-done.1
  2.3 177.4 %shard_map.50 = (bf16[32,2048]{1,0:T(8,128)(2,1)S(1)}, bf16[32,2048]{1,0:T(8,128)(2,1)S(1)}) custom-call(bf16[2048,2048]{1,0:T(8,128)(2,1)} %geno_ref.1, f32[1,2048]{1,0:T(1,128)S(1)} %bitcast.1, f32[32,2048]{1,0:T(8,128)S(1)} %copy-done), custom_call_target="tpu_custom_call" | custom-call | tf_op jit(solution)/shard_map/pallas_call | solution.py:391
  179.7 0.7 copy.7
  180.3 0.7 copy.8
Async XLA Ops:
  0.6 1.0 copy-start
  1.6 0.7 copy-start.1
